TPU v7x, 256 devices: a whole 4x4x8 slice. The times are simulated.
256 devices in a mesh: rows: 64 (over z, y, core), rep: 4 (over x).
Axes of the slice: x: 4, y: 4, z: 8, core: 2. Of those that a mesh axis runs over, the one named last changes fastest.
Arguments:
- features: bfloat16 [262144, 256], P(('rows', 'rep')), may hold values from -6 to 6
- weight: bfloat16 [256, 256], replicated, may hold values from -0.375 to 0.375
- block_cols: int32 [2048, 4, 2], P('rows', 'rep'), may hold values from 0 to 511, as said below
- block_vals: bfloat16 [2048, 4, 2, 128, 128], P('rows', 'rep'), as said below
- out_grad: bfloat16 [262144, 256], P('rows'), may hold values from -6 to 6
Outputs:
- activations: bfloat16 [262144, 256], P(('rows', 'rep'))
- input_grad: bfloat16 [262144, 256], P(('rows', 'rep'))
- weight_grad: float32 [256, 256], replicated
Inputs may be any that keep to these rules, and one draw needn't show every extreme that they name: `block_cols`: layer c's k-th block column is global block column (k // 8) * 32 + c * 8 + k % 8, whose rows the device of index k // 8 along rows holds in layer c. In the layer that owns a block row, slot 0 is its diagonal block; no other held block of a device lies in its own block columns. For every layer, every device along rows and every other device along rows, at most 1 of the first device's held blocks in that layer lie in block columns of the other, and in every draw some pair has exactly 1. `block_vals`: the adjacency is symmetric: every held block at block row b, block column g in slot s has a partner held at block row g, block column b in slot s (of the layer owning b) that is its transpose; diagonal blocks are symmetric.
All inputs are finite; a program needn't handle non-finite values.
Results may differ from a plain program's by a relative error of at most 0.006.
Values may be sent and summed in bfloat16 or wider, within the bound.
A program may use at most 128 MiB of HBM per device.

v0:
```python
import math
import jax
import jax.numpy as jnp
from jax import lax
from jax.sharding import PartitionSpec as P


def silu_parts(summed):
    sigmoid_vals = jax.nn.sigmoid(summed)
    return (summed * sigmoid_vals, sigmoid_vals * (1.0 + summed * (1.0 - sigmoid_vals)))


def apply_blocks(local_vals, fetched):
    product = jnp.einsum("bsij,bsjf->bif", local_vals, fetched, preferred_element_type=jnp.float32)
    return product.reshape(-1, fetched.shape[-1])


def serve_blocks(source_rows, asked_places, block_size):
    feature_width = source_rows.shape[1]
    blocks = source_rows.reshape(-1, block_size, feature_width)
    flat_ask = asked_places.reshape(-1)
    picked = jnp.take(blocks, jnp.clip(flat_ask, 0, blocks.shape[0] - 1), axis=0)
    picked = jnp.where((flat_ask >= 0)[:, None, None], picked, jnp.zeros_like(picked))
    return picked


def on_device(features, weight, block_cols, block_vals, out_grad):
    own_rows, feature_width = features.shape
    block_size = block_vals.shape[-1]
    row_blocks, slot_count = (block_cols.shape[0], block_cols.shape[2])
    own_blocks = own_rows // block_size
    peer_count = lax.axis_size("rows")
    layer_count = lax.axis_size("rep")
    couple_total = ((layer_count - 1) * slot_count * own_blocks + own_blocks) // 2
    reach_classes = peer_count // 2 - 1
    capacity = (couple_total + reach_classes - 1) // reach_classes
    my_group = lax.axis_index("rows")
    layer_index = lax.axis_index("rep")
    local_vals = block_vals[:, 0]
    flat_cols = block_cols[:, 0].reshape(-1)
    request_total = flat_cols.shape[0]
    owners = flat_cols // own_blocks
    places = flat_cols % own_blocks
    remote = owners != my_group
    positions = jnp.arange(request_total, dtype=jnp.int32)
    same_owner = (owners[:, None] == owners[None, :]) & (positions[:, None] > positions[None, :])
    owner_ranks = jnp.sum(same_owner.astype(jnp.int32), axis=1)
    slot_keys = jnp.where(remote, owners * capacity + owner_ranks, -1)
    slot_table = jnp.arange(peer_count * capacity, dtype=jnp.int32)
    matches = slot_keys[:, None] == slot_table[None, :]
    requests = (jnp.sum(jnp.where(matches, places[:, None] + 1, 0), axis=0) - 1).reshape(
        peer_count, capacity
    )
    asked_places = lax.all_to_all(requests, "rows", split_axis=0, concat_axis=0, tiled=True)
    mixed_rows = jnp.dot(features, weight, preferred_element_type=jnp.float32).astype(jnp.bfloat16)
    arrived = lax.all_to_all(
        serve_blocks(mixed_rows, asked_places, block_size),
        "rows",
        split_axis=0,
        concat_axis=0,
        tiled=True,
    )
    from_peers = jnp.take(arrived, jnp.clip(slot_keys, 0, arrived.shape[0] - 1), axis=0)
    from_self = jnp.take(mixed_rows.reshape(own_blocks, block_size, feature_width), places, axis=0)
    joined = jnp.where(remote[:, None, None], from_peers, from_self)
    partial_sum = apply_blocks(
        local_vals, joined.reshape(row_blocks, slot_count, block_size, feature_width)
    )
    share_start = layer_index * own_rows
    summed = lax.psum(partial_sum, "rep")
    values_all, slopes_all = silu_parts(summed)
    grad_rows = (out_grad.astype(jnp.float32) * slopes_all).astype(jnp.bfloat16)
    activated = lax.dynamic_slice_in_dim(values_all, share_start, own_rows, 0).astype(jnp.bfloat16)
    slot_terms = jnp.einsum(
        "bsji,bjf->bsif",
        local_vals,
        grad_rows.reshape(row_blocks, block_size, feature_width),
        preferred_element_type=jnp.float32,
    ).reshape(request_total, block_size, feature_width)
    filler = jnp.sum(jnp.where(matches, positions[:, None], 0), axis=0)
    filled = jnp.any(matches, axis=0)
    outgoing = jnp.where(
        filled[:, None, None], jnp.take(slot_terms, filler, axis=0), jnp.zeros((), jnp.float32)
    )
    returned = lax.all_to_all(outgoing, "rows", split_axis=0, concat_axis=0, tiled=True)
    block_span = block_size * feature_width
    own_index = jnp.arange(own_blocks, dtype=jnp.int32)
    arrive_hot = (asked_places.reshape(-1)[:, None] == own_index[None, :]).astype(jnp.float32)
    self_hot = ((~remote)[:, None] & (places[:, None] == own_index[None, :])).astype(jnp.float32)
    collected = jnp.einsum(
        "qo,qx->ox", arrive_hot, returned.reshape(-1, block_span), precision=lax.Precision.HIGHEST
    )
    self_terms = jnp.einsum(
        "no,nx->ox", self_hot, slot_terms.reshape(-1, block_span), precision=lax.Precision.HIGHEST
    )
    back_rows = (collected + self_terms).reshape(own_rows, feature_width)
    node_total = own_rows * peer_count * layer_count
    local_weight = jnp.dot(
        features.astype(jnp.float32).T, back_rows, precision=lax.Precision.HIGHEST
    )
    weight_grad = lax.psum(local_weight, ("rows", "rep")) * (1.0 / math.sqrt(node_total))
    input_grad = jnp.dot(
        back_rows.astype(jnp.bfloat16), weight.T, preferred_element_type=jnp.float32
    ).astype(jnp.bfloat16)
    return (activated, input_grad, weight_grad)


def solution(mesh):
    placed = (
        P(("rows", "rep"), None),
        P(),
        P("rows", "rep", None),
        P("rows", "rep", None, None, None),
        P("rows", None),
    )
    return jax.shard_map(
        on_device,
        mesh=mesh,
        in_specs=placed,
        out_specs=(P(("rows", "rep"), None), P(("rows", "rep"), None), P()),
        check_vma=False,
    )
```

profile of v0, /device:TPU:2, one launch (start us, length us, event | category | flops | bytes accessed | tf_op | source)
XLA Modules:
  0.0 755.1 jit_solution(3216159301547902736)
XLA Ops:
  7.2 0.9 copy.37
  9.3 12.1 %all-to-all-start = ((s32[64,1,1]{2,1,0:T(1,128)}), s32[64,1,1]{2,1,0:T(1,128)S(1)}, u32[]{:S(2)}, u32[]{:S(2)}) async-start(s32[64,1,1]{2,1,0:T(1,128)} %copy.38), calls=%async_computation | async-start | bytes 65536 | tf_op jit(solution)/shard_map/all_to_all | solution.py:54
  21.4 1.4 convolution_convert_fusion.1
  22.7 8.2 %all-to-all-done = s32[64,1,1]{2,1,0:T(1,128)S(1)} async-done(((s32[64,1,1]{2,1,0:T(1,128)}), s32[64,1,1]{2,1,0:T(1,128)S(1)}, u32[]{:S(2)}, u32[]{:S(2)}) %all-to-all-start) | async-done | bytes 288 | tf_op jit(solution)/shard_map/all_to_all | solution.py:54
  30.9 1.2 reduce.1
  32.1 2.8 gather_fusion.2
  34.9 1.2 compare_reduce_fusion
  36.1 4.0 select_select_fusion.2
  40.1 5.7 all-to-all-start.1
  46.1 2.8 gather_fusion.3
  48.9 93.1 %all-to-all-done.1 = bf16[64,128,256]{2,1,0:T(8,128)(2,1)} async-done(((bf16[64,128,256]{2,1,0:T(8,128)(2,1)}), bf16[64,128,256]{2,1,0:T(8,128)(2,1)}, u32[]{:S(2)}, u32[]{:S(2)}) %all-to-all-start.1) | async-done | bytes 4194336 | tf_op jit(solution)/shard_map/all_to_all | solution.py:56
  142.0 5.0 gather_fusion
  147.0 4.1 select_select_fusion.1
  151.0 2.8 fusion.2
  154.0 92.9 %all-reduce.3.cloned.1.call-done = f32[4096,256]{1,0:T(8,128)} async-done(((f32[4096,256]{1,0:T(8,128)}), f32[4096,256]{1,0:T(8,128)}) %all-reduce.3.cloned.1.call-update) | async-done | bytes 4194320 | tf_op jit(solution)/shard_map/psum | solution.py:70
  246.9 6.4 multiply_convert_fusion
  253.3 4.5 fusion
  257.9 9.0 %copy.41 = f32[64,128,256]{2,1,0:T(8,128)} copy(f32[64,128,256]{1,2,0:T(8,128)} %bitcast.59) | data formatting | bytes 16777216 | tf_op jit(solution)/shard_map/reshape | solution.py:79
  266.9 7.7 %gather_fusion.1 = f32[64,128,256]{2,1,0:T(8,128)} fusion(f32[64,128,256]{2,1,0:T(8,128)} %copy.41, s32[1024]{0:T(1024)S(1)} %pad_clamp_fusion), kind=kCustom, calls=%fused_computation.3 | custom fusion | bytes 16777472 | tf_op jit(solution)/shard_map/jit(_take)/gather | solution.py:83
  274.5 8.5 %select_select_fusion = f32[64,128,256]{2,1,0:T(8,128)} fusion(f32[64,128,256]{2,1,0:T(8,128)} %gather_fusion.1, pred[64]{0:T(512)(128)(4,1)S(1)} %compare_and_fusion.2, pred[64]{0:T(512)(128)(4,1)S(1)} %fusion.6), kind=kLoop, calls=%fused_computation.5 | loop fusion | flops 4194304 | bytes 16777344 | tf_op jit(solution)/shard_map/jit(_where)/select_n | solution.py:82
  283.0 10.7 %all-to-all-start.2 = ((f32[64,128,256]{2,1,0:T(8,128)}), f32[64,128,256]{2,1,0:T(8,128)}, u32[]{:S(2)}, u32[]{:S(2)}) async-start(f32[64,128,256]{2,1,0:T(8,128)} %select_select_fusion), calls=%async_computation.2 | async-start | bytes 16777216 | tf_op jit(solution)/shard_map/all_to_all | solution.py:85
  293.8 9.2 %copy.49 = f32[8,8,128,256]{3,1,2,0:T(8,128)} copy(f32[8,8,128,256]{2,3,1,0:T(8,128)} %bitcast.60) | data formatting | bytes 16777216
  303.0 2.4 fusion.4
  305.5 174.4 %all-to-all-done.2 = f32[64,128,256]{2,1,0:T(8,128)} async-done(((f32[64,128,256]{2,1,0:T(8,128)}), f32[64,128,256]{2,1,0:T(8,128)}, u32[]{:S(2)}, u32[]{:S(2)}) %all-to-all-start.2) | async-done | bytes 8388640 | tf_op jit(solution)/shard_map/all_to_all | solution.py:85
  479.9 8.3 %copy.48 = f32[8,8,128,256]{3,1,2,0:T(8,128)S(1)} copy(f32[8,8,128,256]{3,2,1,0:T(8,128)} %bitcast.25) | data formatting | bytes 16777216
  488.1 2.9 fusion.8
  491.1 3.9 convolution_add_fusion
  494.9 1.4 reshape.298
  496.4 2.7 convolution_bitcast_fusion
  499.1 1.1 convolution_convert_fusion
  500.3 246.2 %all-reduce.5.cloned.1.call-done = f32[256,256]{0,1:T(8,128)} async-done(((f32[256,256]{0,1:T(8,128)}), f32[256,256]{0,1:T(8,128)}) %all-reduce.5.cloned.1.call-update) | async-done | bytes 262160 | tf_op jit(solution)/shard_map/psum | solution.py:101
  746.4 1.0 broadcast_multiply_fusion
  (34 shorter events, 2.6 us)
Async XLA Ops:
  7.2 143.9 %copy-start = (bf16[32,1,2,128,128]{4,3,2,1,0:T(8,128)(2,1)S(1)}, bf16[32,1,2,128,128]{4,3,2,1,0:T(8,128)(2,1)}, u32[]{:S(2)}) copy-start(bf16[32,1,2,128,128]{4,3,2,1,0:T(8,128)(2,1)} %param.10) | copy-start | bytes 6291460
  9.3 21.6 %all-to-all-start = ((s32[64,1,1]{2,1,0:T(1,128)}), s32[64,1,1]{2,1,0:T(1,128)S(1)}, u32[]{:S(2)}, u32[]{:S(2)}) async-start(s32[64,1,1]{2,1,0:T(1,128)} %copy.38), calls=%async_computation | async-start | bytes 65536 | tf_op jit(solution)/shard_map/all_to_all | solution.py:54
  40.1 101.9 %all-to-all-start.1 = ((bf16[64,128,256]{2,1,0:T(8,128)(2,1)}), bf16[64,128,256]{2,1,0:T(8,128)(2,1)}, u32[]{:S(2)}, u32[]{:S(2)}) async-start(bf16[64,128,256]{2,1,0:T(8,128)(2,1)} %select_select_fusion.2), calls=%async_computation.1 | async-start | bytes 8388608 | tf_op jit(solution)/shard_map/all_to_all | solution.py:56
  45.8 201.1 %all-reduce.3.cloned.1.call-start = ((), (), s32[]{:S(2)}) async-start(), calls=%async_computation.3 | async-start | bytes 8388608 | tf_op jit(solution)/shard_map/psum | solution.py:70
  283.0 196.8 %all-to-all-start.2 = ((f32[64,128,256]{2,1,0:T(8,128)}), f32[64,128,256]{2,1,0:T(8,128)}, u32[]{:S(2)}, u32[]{:S(2)}) async-start(f32[64,128,256]{2,1,0:T(8,128)} %select_select_fusion), calls=%async_computation.2 | async-start | bytes 16777216 | tf_op jit(solution)/shard_map/all_to_all | solution.py:85
  293.8 452.7 %all-reduce.5.cloned.1.call-start = ((), (), s32[]{:S(2)}) async-start(), calls=%async_computation.4 | async-start | bytes 524288 | tf_op jit(solution)/shard_map/psum | solution.py:101
  479.8 11.2 %slice-start = ((s8[8388608]{0:T(1024)(128)(4,1)}), s8[4194304]{0:T(1024)(128)(4,1)S(1)}, s32[]{:S(2)}) async-start(s8[8388608]{0:T(1024)(128)(4,1)} %bitcast.63), calls=%async_computation.5 | async-start | bytes 8388608
  479.9 11.2 %slice-start.1 = ((s8[8388608]{0:T(1024)(128)(4,1)}), s8[4194304]{0:T(1024)(128)(4,1)S(1)}, s32[]{:S(2)}) async-start(s8[8388608]{0:T(1024)(128)(4,1)} %bitcast.63), calls=%async_computation.6 | async-start | bytes 8388608
  491.0 257.2 %copy-start.1 = (bf16[32,1,2,128,128]{4,3,2,1,0:T(8,128)(2,1)S(1)}, bf16[32,1,2,128,128]{4,3,2,1,0:T(8,128)(2,1)}, u32[]{:S(2)}) copy-start(bf16[32,1,2,128,128]{4,3,2,1,0:T(8,128)(2,1)} %param.10) | copy-start | bytes 6291460
  494.9 4.2 copy-start.2
Sparse Core Ops, SparseCore 0:
  154.0 92.8 all-reduce.2
  499.2 247.1 all-reduce.4
where the time goes:
time: 756 us; the launch traced here: 755 us
  waiting for transfers between devices  615 us (81%)
  local copies, waits for them, and re-layouts  48.7 us (6%)
  other arithmetic  29.3 us (4%)
  starting transfers between devices  28.8 us (4%)
  matrix products  19.3 us (3%)
  between operations  14.2 us (2%)
    psum x1, waiting for transfers between devices, on_device(): lax.psum(local_weight, ('rows', 'rep')) * (1.0 / math.sqrt(node_total))  246 us
    all_to_all x1, waiting for transfers between devices, on_device(): lax.all_to_all(outgoing, 'rows', split_axis=0, concat_axis=0, tiled=True)  174 us
    all_to_all x1, waiting for transfers between devices, on_device(): lax.all_to_all(serve_blocks(mixed_rows, asked_places, block_size), 'rows'...  93.1 us
    psum x1, waiting for transfers between devices, on_device(): summed = lax.psum(partial_sum, 'rep')  92.9 us
    unnamed x14, local copies, waits for them, and re-layouts  19.2 us
  transfers between devices with their start and end apart: 5, of which 5 were waited for; matrix products, arithmetic and copies ran while one was open for 2% of the time, Pallas kernels for 0%

commit v1 on v0

--- a/solution.py
+++ b/solution.py
@@ -25,6 +25,12 @@
 
 
 def on_device(features, weight, block_cols, block_vals, out_grad):
+
+    def watch_tails_now(body):
+        for k0 in ("rep", "rows"):
+            body = jax.lax.psum(body, axis_name=k0)
+        return body
+
     own_rows, feature_width = features.shape
     block_size = block_vals.shape[-1]
     row_blocks, slot_count = (block_cols.shape[0], block_cols.shape[2])
@@ -98,7 +104,7 @@
     local_weight = jnp.dot(
         features.astype(jnp.float32).T, back_rows, precision=lax.Precision.HIGHEST
     )
-    weight_grad = lax.psum(local_weight, ("rows", "rep")) * (1.0 / math.sqrt(node_total))
+    weight_grad = watch_tails_now(local_weight) * (1.0 / math.sqrt(node_total))
     input_grad = jnp.dot(
         back_rows.astype(jnp.bfloat16), weight.T, preferred_element_type=jnp.float32
     ).astype(jnp.bfloat16)

time: 756 us -> 732 us (0.968)
  waiting for transfers between devices: 615 us -> 589 us
    psum x1 -> x2, waiting for transfers between devices: 246 us -> 218 us  [watch_tails_now(): body = jax.lax.psum(body, axis_name=k0)]
  transfers between devices with their start and end apart: 5 -> 6, of which waited for: 5 -> 6; matrix products, arithmetic and copies ran while one was open for 2% -> 2% of each run, Pallas kernels for 0% -> 0%
where the time goes in v1:
time: 732 us; the launch traced here: 729 us
  waiting for transfers between devices  589 us (80%)
  local copies, waits for them, and re-layouts  48.9 us (7%)
  other arithmetic  29.3 us (4%)
  starting transfers between devices  28.8 us (4%)
  matrix products  19.3 us (3%)
  between operations  13.9 us (2%)
    psum x2, waiting for transfers between devices, watch_tails_now(): body = jax.lax.psum(body, axis_name=k0)  218 us
    all_to_all x1, waiting for transfers between devices, on_device(): lax.all_to_all(outgoing, 'rows', split_axis=0, concat_axis=0, tiled=True)  177 us
    all_to_all x1, waiting for transfers between devices, on_device(): lax.all_to_all(serve_blocks(mixed_rows, asked_places, block_size), 'rows'...  93.1 us
    psum x1, waiting for transfers between devices, on_device(): summed = lax.psum(partial_sum, 'rep')  92.9 us
    unnamed x14, local copies, waits for them, and re-layouts  19.2 us
  transfers between devices with their start and end apart: 6, of which 6 were waited for; matrix products, arithmetic and copies ran while one was open for 2% of the time, Pallas kernels for 0%

profile of v1, /device:TPU:2, one launch (start us, length us, event | category | flops | bytes accessed | tf_op | source)
XLA Modules:
  0.0 729.1 jit_solution(2726750308626880181)
XLA Ops:
  9.3 12.1 %all-to-all-start = ((s32[64,1,1]{2,1,0:T(1,128)}), s32[64,1,1]{2,1,0:T(1,128)S(1)}, u32[]{:S(2)}, u32[]{:S(2)}) async-start(s32[64,1,1]{2,1,0:T(1,128)} %copy.38), calls=%async_computation | async-start | bytes 65536 | tf_op jit(solution)/shard_map/all_to_all | solution.py:60
  21.4 1.4 convolution_convert_fusion.1
  22.7 8.2 %all-to-all-done = s32[64,1,1]{2,1,0:T(1,128)S(1)} async-done(((s32[64,1,1]{2,1,0:T(1,128)}), s32[64,1,1]{2,1,0:T(1,128)S(1)}, u32[]{:S(2)}, u32[]{:S(2)}) %all-to-all-start) | async-done | bytes 288 | tf_op jit(solution)/shard_map/all_to_all | solution.py:60
  30.9 1.2 reduce.1
  32.1 2.8 gather_fusion.2
  34.9 1.2 compare_reduce_fusion
  36.1 4.0 select_select_fusion.2
  40.1 5.7 all-to-all-start.1
  46.1 2.8 gather_fusion.3
  48.9 93.1 %all-to-all-done.1 = bf16[64,128,256]{2,1,0:T(8,128)(2,1)} async-done(((bf16[64,128,256]{2,1,0:T(8,128)(2,1)}), bf16[64,128,256]{2,1,0:T(8,128)(2,1)}, u32[]{:S(2)}, u32[]{:S(2)}) %all-to-all-start.1) | async-done | bytes 4194336 | tf_op jit(solution)/shard_map/all_to_all | solution.py:62
  142.0 5.0 gather_fusion
  147.0 4.1 select_select_fusion.1
  151.0 2.8 fusion.2
  154.0 92.9 %all-reduce.4.cloned.1.call-done = f32[4096,256]{1,0:T(8,128)} async-done(((f32[4096,256]{1,0:T(8,128)}), f32[4096,256]{1,0:T(8,128)}) %all-reduce.4.cloned.1.call-update) | async-done | bytes 4194320 | tf_op jit(solution)/shard_map/psum | solution.py:76
  246.9 6.4 multiply_convert_fusion
  253.3 4.5 fusion
  257.9 9.0 %copy.41 = f32[64,128,256]{2,1,0:T(8,128)} copy(f32[64,128,256]{1,2,0:T(8,128)} %bitcast.59) | data formatting | bytes 16777216 | tf_op jit(solution)/shard_map/reshape | solution.py:85
  266.9 7.7 %gather_fusion.1 = f32[64,128,256]{2,1,0:T(8,128)} fusion(f32[64,128,256]{2,1,0:T(8,128)} %copy.41, s32[1024]{0:T(1024)S(1)} %pad_clamp_fusion), kind=kCustom, calls=%fused_computation.3 | custom fusion | bytes 16777472 | tf_op jit(solution)/shard_map/jit(_take)/gather | solution.py:89
  274.5 8.5 %select_select_fusion = f32[64,128,256]{2,1,0:T(8,128)} fusion(f32[64,128,256]{2,1,0:T(8,128)} %gather_fusion.1, pred[64]{0:T(512)(128)(4,1)S(1)} %compare_and_fusion.2, pred[64]{0:T(512)(128)(4,1)S(1)} %fusion.6), kind=kLoop, calls=%fused_computation.5 | loop fusion | flops 4194304 | bytes 16777344 | tf_op jit(solution)/shard_map/jit(_where)/select_n | solution.py:88
  283.0 10.7 %all-to-all-start.2 = ((f32[64,128,256]{2,1,0:T(8,128)}), f32[64,128,256]{2,1,0:T(8,128)}, u32[]{:S(2)}, u32[]{:S(2)}) async-start(f32[64,128,256]{2,1,0:T(8,128)} %select_select_fusion), calls=%async_computation.2 | async-start | bytes 16777216 | tf_op jit(solution)/shard_map/all_to_all | solution.py:91
  293.8 9.2 %copy.49 = f32[8,8,128,256]{3,1,2,0:T(8,128)} copy(f32[8,8,128,256]{2,3,1,0:T(8,128)} %bitcast.60) | data formatting | bytes 16777216
  303.0 176.8 %all-to-all-done.2 = f32[64,128,256]{2,1,0:T(8,128)} async-done(((f32[64,128,256]{2,1,0:T(8,128)}), f32[64,128,256]{2,1,0:T(8,128)}, u32[]{:S(2)}, u32[]{:S(2)}) %all-to-all-start.2) | async-done | bytes 8388640 | tf_op jit(solution)/shard_map/all_to_all | solution.py:91
  479.9 8.3 %copy.48 = f32[8,8,128,256]{3,1,2,0:T(8,128)S(1)} copy(f32[8,8,128,256]{3,2,1,0:T(8,128)} %bitcast.25) | data formatting | bytes 16777216
  488.1 2.9 fusion.8
  491.0 3.9 convolution_add_fusion
  494.9 1.5 reshape.298
  496.5 2.7 convolution_bitcast_fusion
  499.3 2.4 fusion.4
  501.7 40.2 %all-reduce.6.cloned.1.call-done = f32[256,256]{0,1:T(8,128)} async-done(((f32[256,256]{0,1:T(8,128)}), f32[256,256]{0,1:T(8,128)}) %all-reduce.6.cloned.1.call-update) | async-done | bytes 262160 | tf_op jit(solution)/shard_map/psum | solution.py:31
  541.9 1.1 convolution_convert_fusion
  543.1 177.7 %all-reduce.8.cloned.1.call-done = f32[256,256]{0,1:T(8,128)} async-done(((f32[256,256]{0,1:T(8,128)}), f32[256,256]{0,1:T(8,128)}) %all-reduce.8.cloned.1.call-update) | async-done | bytes 262160 | tf_op jit(solution)/shard_map/psum | solution.py:31
  720.8 1.0 broadcast_multiply_fusion
  (37 shorter events, 3.5 us)
Async XLA Ops:
  7.2 143.9 %copy-start = (bf16[32,1,2,128,128]{4,3,2,1,0:T(8,128)(2,1)S(1)}, bf16[32,1,2,128,128]{4,3,2,1,0:T(8,128)(2,1)}, u32[]{:S(2)}) copy-start(bf16[32,1,2,128,128]{4,3,2,1,0:T(8,128)(2,1)} %param.10) | copy-start | bytes 6291460
  9.3 21.6 %all-to-all-start = ((s32[64,1,1]{2,1,0:T(1,128)}), s32[64,1,1]{2,1,0:T(1,128)S(1)}, u32[]{:S(2)}, u32[]{:S(2)}) async-start(s32[64,1,1]{2,1,0:T(1,128)} %copy.38), calls=%async_computation | async-start | bytes 65536 | tf_op jit(solution)/shard_map/all_to_all | solution.py:60
  40.1 101.9 %all-to-all-start.1 = ((bf16[64,128,256]{2,1,0:T(8,128)(2,1)}), bf16[64,128,256]{2,1,0:T(8,128)(2,1)}, u32[]{:S(2)}, u32[]{:S(2)}) async-start(bf16[64,128,256]{2,1,0:T(8,128)(2,1)} %select_select_fusion.2), calls=%async_computation.1 | async-start | bytes 8388608 | tf_op jit(solution)/shard_map/all_to_all | solution.py:62
  45.8 201.1 %all-reduce.4.cloned.1.call-start = ((), (), s32[]{:S(2)}) async-start(), calls=%async_computation.3 | async-start | bytes 8388608 | tf_op jit(solution)/shard_map/psum | solution.py:76
  283.0 196.8 %all-to-all-start.2 = ((f32[64,128,256]{2,1,0:T(8,128)}), f32[64,128,256]{2,1,0:T(8,128)}, u32[]{:S(2)}, u32[]{:S(2)}) async-start(f32[64,128,256]{2,1,0:T(8,128)} %select_select_fusion), calls=%async_computation.2 | async-start | bytes 16777216 | tf_op jit(solution)/shard_map/all_to_all | solution.py:91
  293.8 248.1 %all-reduce.6.cloned.1.call-start = ((), (), s32[]{:S(2)}) async-start(), calls=%async_computation.4 | async-start | bytes 524288 | tf_op jit(solution)/shard_map/psum | solution.py:31
  479.8 11.2 %slice-start = ((s8[8388608]{0:T(1024)(128)(4,1)}), s8[4194304]{0:T(1024)(128)(4,1)S(1)}, s32[]{:S(2)}) async-start(s8[8388608]{0:T(1024)(128)(4,1)} %bitcast.63), calls=%async_computation.6 | async-start | bytes 8388608
  479.9 11.2 %slice-start.1 = ((s8[8388608]{0:T(1024)(128)(4,1)}), s8[4194304]{0:T(1024)(128)(4,1)S(1)}, s32[]{:S(2)}) async-start(s8[8388608]{0:T(1024)(128)(4,1)} %bitcast.63), calls=%async_computation.7 | async-start | bytes 8388608
  494.9 47.0 %copy-start.2 = (bf16[256,256]{1,0:T(8,128)(2,1)S(1)}, bf16[256,256]{1,0:T(8,128)(2,1)}, u32[]{:S(2)}) copy-start(bf16[256,256]{1,0:T(8,128)(2,1)} %param.8) | copy-start | bytes 393220
  494.9 227.7 %copy-start.1 = (bf16[32,1,2,128,128]{4,3,2,1,0:T(8,128)(2,1)S(1)}, bf16[32,1,2,128,128]{4,3,2,1,0:T(8,128)(2,1)}, u32[]{:S(2)}) copy-start(bf16[32,1,2,128,128]{4,3,2,1,0:T(8,128)(2,1)} %param.10) | copy-start | bytes 6291460
  499.2 221.6 %all-reduce.8.cloned.1.call-start = ((), (), s32[]{:S(2)}) async-start(), calls=%async_computation.5 | async-start | bytes 524288 | tf_op jit(solution)/shard_map/psum | solution.py:31
Sparse Core Ops, SparseCore 0:
  154.0 92.8 all-reduce.3
  499.4 42.4 all-reduce.5
  545.4 175.3 all-reduce.7
